TPU v7x, 32 devices: a whole 2x2x4 slice. The times are simulated.
32 devices in a mesh: groups: 2 (over y), seq: 4 (over z), section: 2 (over x), tp: 2 (over core).
Axes of the slice: x: 2, y: 2, z: 4, core: 2. Of those that a mesh axis runs over, the one named last changes fastest.
Arguments:
- hidden_in: bfloat16 [16, 8192], P('groups', ('seq', 'section', 'tp')), parts along dimension 0, may hold values from -6 to 6
- lengths: int32 [16], P('groups'), parts along dimension 0, may hold values from 1 to 512, as said below
- key_value_cache: bfloat16 [16, 2, 512, 1024], P('groups', None, 'seq', ('section', 'tp')), parts along dimension 0, may hold values from -900 to 900
- attn_gain: float32 [8192], P('seq'), may hold values from 0.1 to 1.9
- w_query: bfloat16 [8192, 8192], P('seq', ('section', 'tp')), may hold values from -0.0625 to 0.0625
- key_value_weight: bfloat16 [8192, 2, 1024], P('seq', None, ('section', 'tp')), may hold values from -0.0625 to 0.0625
- w_output: bfloat16 [8192, 8192], P(('section', 'tp'), 'seq'), may hold values from -0.0625 to 0.0625
- mamba_gain: float32 [8192], P('seq'), may hold values from 0.1 to 1.9
- w_inproj: bfloat16 [8192, 2, 16384], P('seq', None, ('section', 'tp')), may hold values from -0.09375 to 0.09375
- conv_weight: float32 [4, 16384], P(None, ('section', 'tp', 'seq')), may hold values from -3 to 3
- conv_bias: float32 [16384], P(('section', 'tp', 'seq')), may hold values from -3 to 3
- w_xproj: bfloat16 [16384, 544], P(('section', 'tp', 'seq')), may hold values from -0.046875 to 0.046875
- w_dtproj: bfloat16 [512, 16384], P(None, ('section', 'tp', 'seq')), may hold values from -0.25 to 0.25
- dt_bias: float32 [16384], P(('section', 'tp', 'seq')), may hold values from -4 to 0
- a_log: float32 [16, 16384], P(None, ('section', 'tp', 'seq')), may hold values from 0 to 2.77
- d_skip: float32 [16384], P(('section', 'tp', 'seq')), may hold values from 0.25 to 2
- w_outproj: bfloat16 [16384, 8192], P(('section', 'tp'), 'seq'), may hold values from -0.046875 to 0.046875
- ssm_state: float32 [16, 16, 16384], P('groups', None, ('section', 'tp', 'seq')), parts along dimension 0, may hold values from -6 to 6
- conv_window: bfloat16 [16, 3, 16384], P('groups', None, ('section', 'tp', 'seq')), parts along dimension 0, may hold values from -6 to 6
Outputs:
- hidden_out: bfloat16 [16, 8192], P('groups', ('seq', 'section', 'tp')), parts along dimension 0
- state_out: float32 [16, 16, 16384], P('groups', None, ('section', 'tp', 'seq')), parts along dimension 0
- window_out: bfloat16 [16, 3, 16384], P('groups', None, ('section', 'tp', 'seq')), parts along dimension 0
There are 2 independent parts, one for each index of `groups`. A program takes and returns all parts, laid end to end along the dimension named above; an argument that names none is the same for every part. Nothing has to cross between parts.
Inputs may be any that keep to these rules, and one draw needn't show every extreme that they name: `lengths`: the new token sits after the cached positions; one sequence of every draw has exactly 512; where there are two or more sequences, one or two others have at most 16.
All inputs are finite; a program needn't handle non-finite values.
Results may differ from a plain program's by a relative error of at most 0.012.
Values may be sent and summed in bfloat16 or wider, within the bound.
No kernel may reach another device: no remote copies, remote signals or barrier semaphores. Data moves between devices by JAX's collectives and lax.ppermute only.
A program may use at most 192 MiB of HBM per device.

v0:
```python
import jax
import jax.numpy as jnp
from jax import lax
from jax.sharding import PartitionSpec as P

MODEL_WIDTH = 8192
QUERY_HEADS = 64
KEY_VALUE_HEADS = 8
HEAD_SIZE = 128
DS = 16
DTR = 512
EPSILON = 1e-06
NEGATIVE = -1e30


def joined(value, axis, join):
    pieces = jax.tree.map(lambda part: lax.all_gather(part, axis), value)
    head = jax.tree.map(lambda part: part[0], pieces)
    tail = jax.tree.map(lambda part: part[1:], pieces)
    subtotal, _ = lax.scan(lambda subtotal, piece: (join(subtotal, piece), None), head, tail)
    return subtotal


def combine_parts(earlier, later):
    first_max, first_sum, first_out = earlier
    second_max, second_sum, second_out = later
    largest = jnp.maximum(first_max, second_max)
    first_factor = jnp.exp(first_max - largest)
    second_factor = jnp.exp(second_max - largest)
    return (
        largest,
        first_sum * first_factor + second_sum * second_factor,
        first_out * first_factor[..., None] + second_out * second_factor[..., None],
    )


def on_device(
    hidden_in,
    lengths,
    key_value_cache,
    attn_gain,
    w_query,
    key_value_weight,
    w_output,
    mamba_gain,
    w_inproj,
    conv_weight,
    conv_bias,
    w_xproj,
    w_dtproj,
    dt_bias,
    a_log,
    d_skip,
    w_outproj,
    ssm_state,
    conv_window,
):
    batch = hidden_in.shape[0]
    seq_index = lax.axis_index("seq")
    query_groups_count = QUERY_HEADS // KEY_VALUE_HEADS
    local_kv = key_value_weight.shape[2] // HEAD_SIZE
    head_cols = local_kv * query_groups_count * HEAD_SIZE
    gathered = lax.all_gather(hidden_in, ("section", "tp"), axis=1, tiled=True)
    wide_in = gathered.astype(jnp.float32)
    normed_input = (wide_in * attn_gain).astype(jnp.bfloat16)
    square_part = jnp.sum(wide_in * wide_in, axis=1)
    query_part = jnp.dot(normed_input, w_query, preferred_element_type=jnp.float32)
    keyval_part = jnp.dot(
        normed_input,
        key_value_weight.reshape(key_value_weight.shape[0], 2 * key_value_weight.shape[2]),
        preferred_element_type=jnp.float32,
    )
    square_sum, query_sum, keyval_sum = lax.psum((square_part, query_part, keyval_part), "seq")
    reciprocal_leading = lax.rsqrt(square_sum / MODEL_WIDTH + EPSILON)
    query_rows_local = (
        (reciprocal_leading[:, None] * query_sum)
        .astype(jnp.bfloat16)
        .reshape(batch, local_kv, query_groups_count, HEAD_SIZE)
    )
    key_value_rows = (
        (reciprocal_leading[:, None] * keyval_sum)
        .astype(jnp.bfloat16)
        .reshape(batch, 2, local_kv, HEAD_SIZE)
    )
    new_key = key_value_rows[:, 0]
    new_value = key_value_rows[:, 1]
    span = key_value_cache.shape[2]
    stored_keys = key_value_cache[:, 0].reshape(batch, span, local_kv, HEAD_SIZE)
    stored_values = key_value_cache[:, 1].reshape(batch, span, local_kv, HEAD_SIZE)
    inv_root = HEAD_SIZE ** (-0.5)
    scores = (
        jnp.einsum(
            "bgrd,btgd->bgrt", query_rows_local, stored_keys, preferred_element_type=jnp.float32
        )
        * inv_root
    )
    position = seq_index * span + jnp.arange(span, dtype=jnp.int32)
    is_valid = (position[None, :] < lengths[:, None])[:, None, None, :]
    masked = jnp.where(is_valid, scores, NEGATIVE)
    local_max = jnp.max(masked, axis=3)
    weights = jnp.where(is_valid, jnp.exp(masked - local_max[..., None]), 0.0)
    local_sum = jnp.sum(weights, axis=3)
    local_out = jnp.einsum(
        "bgrt,btgd->bgrd",
        weights.astype(jnp.bfloat16),
        stored_values,
        preferred_element_type=jnp.float32,
    )
    new_score = (
        jnp.einsum("bgrd,bgd->bgr", query_rows_local, new_key, preferred_element_type=jnp.float32)
        * inv_root
    )
    value_wide = jnp.broadcast_to(
        new_value[:, :, None, :], (batch, local_kv, query_groups_count, HEAD_SIZE)
    ).astype(jnp.float32)
    new_part = (new_score, jnp.ones_like(new_score), value_wide)
    merged = joined((local_max, local_sum, local_out), "seq", combine_parts)
    top_score, denominator, numerator = combine_parts(merged, new_part)
    attended = (numerator / denominator[..., None]).astype(jnp.bfloat16).reshape(batch, head_cols)
    attn_part = jnp.dot(attended, w_output, preferred_element_type=jnp.float32)
    attn_piece = lax.psum_scatter(attn_part, ("section", "tp"), scatter_dimension=1, tiled=True)
    hidden_mid = (hidden_in.astype(jnp.float32) + attn_piece).astype(jnp.bfloat16)
    mid_rows = lax.all_gather(hidden_mid, ("section", "tp"), axis=1, tiled=True)
    mid_wide = mid_rows.astype(jnp.float32)
    mid_square = lax.psum(jnp.sum(mid_wide * mid_wide, axis=1), "seq")
    inv_second = lax.rsqrt(mid_square / MODEL_WIDTH + EPSILON)
    scaled_mid = (mid_wide * mamba_gain).astype(jnp.bfloat16)
    in_rows = w_inproj.shape[0]
    local_inner = w_inproj.shape[2]
    both_term = jnp.dot(
        scaled_mid, w_inproj.reshape(in_rows, 2 * local_inner), preferred_element_type=jnp.float32
    ).reshape(batch, 2, local_inner)
    both_sum = lax.psum_scatter(both_term, "seq", scatter_dimension=2, tiled=True)
    conv_sum = both_sum[:, 0]
    gate_sum = both_sum[:, 1]
    conv_input = (inv_second[:, None] * conv_sum).astype(jnp.bfloat16)
    window = jnp.concatenate([conv_window, conv_input[:, None, :]], axis=1)
    conv_out = conv_bias + jnp.sum(conv_weight[None] * window.astype(jnp.float32), axis=1)
    conv_act = jax.nn.silu(conv_out).astype(jnp.bfloat16)
    xproj_out = lax.psum(
        jnp.dot(conv_act, w_xproj, preferred_element_type=jnp.float32), ("seq", "section", "tp")
    )
    rate_low = xproj_out[:, :DTR].astype(jnp.bfloat16)
    input_proj = xproj_out[:, DTR : DTR + DS]
    output_proj = xproj_out[:, DTR + DS :]
    step_size = jax.nn.softplus(
        jnp.dot(rate_low, w_dtproj, preferred_element_type=jnp.float32) + dt_bias
    )
    decays = jnp.exp(-step_size[:, None, :] * jnp.exp(a_log)[None])
    conv_wide = conv_act.astype(jnp.float32)
    state_out = (
        decays * ssm_state + step_size[:, None, :] * input_proj[:, :, None] * conv_wide[:, None, :]
    )
    readout = jnp.sum(output_proj[:, :, None] * state_out, axis=1) + d_skip * conv_wide
    gate_part = inv_second[:, None] * gate_sum
    gated_out = (readout * jax.nn.silu(gate_part)).astype(jnp.bfloat16)
    mamba_part = jnp.dot(
        lax.all_gather(gated_out, "seq", axis=1, tiled=True),
        w_outproj,
        preferred_element_type=jnp.float32,
    )
    mamba_piece = lax.psum_scatter(mamba_part, ("section", "tp"), scatter_dimension=1, tiled=True)
    hidden_out = (hidden_mid.astype(jnp.float32) + mamba_piece).astype(jnp.bfloat16)
    return (hidden_out, state_out, window[:, 1:])


def solution(mesh):
    return jax.shard_map(
        on_device,
        mesh=mesh,
        in_specs=(
            P("groups", ("seq", "section", "tp")),
            P("groups"),
            P("groups", None, "seq", ("section", "tp")),
            P("seq"),
            P("seq", ("section", "tp")),
            P("seq", None, ("section", "tp")),
            P(("section", "tp"), "seq"),
            P("seq"),
            P("seq", None, ("section", "tp")),
            P(None, ("section", "tp", "seq")),
            P(("section", "tp", "seq")),
            P(("section", "tp", "seq"), None),
            P(None, ("section", "tp", "seq")),
            P(("section", "tp", "seq")),
            P(None, ("section", "tp", "seq")),
            P(("section", "tp", "seq")),
            P(("section", "tp"), "seq"),
            P("groups", None, ("section", "tp", "seq")),
            P("groups", None, ("section", "tp", "seq")),
        ),
        out_specs=(
            P("groups", ("seq", "section", "tp")),
            P("groups", None, ("section", "tp", "seq")),
            P("groups", None, ("section", "tp", "seq")),
        ),
        check_vma=False,
    )
```

profile of v0, /device:TPU:0, one launch (start us, length us, event | category | flops | bytes accessed | tf_op | source)
XLA Modules:
  0.0 326.4 jit_solution(9584996585662456472)
XLA Ops:
  7.2 6.5 %all_gather.27 = bf16[8,2048]{1,0:T(8,128)(2,1)S(1)} all-gather(bf16[8,512]{1,0:T(8,128)(2,1)} %param.21), channel_id=1, replica_groups=mesh['groups'=2,'seq'=4,'section'=2,'tp'=2] {'section','tp'}, dimensions={1}, use_global_device_ids=true | all-gather | bytes 40960 | tf_op jit(solution)/shard_map/all_gather | solution.py:63
  13.8 5.4 %fusion.32 = f32[8,2048]{1,0:T(8,128)} fusion(bf16[2048,2048]{1,0:T(8,128)(2,1)} %param.25, bf16[8,2048]{1,0:T(8,128)(2,1)S(1)} %all_gather.27, f32[2048]{0:T(1024)} %param.24), kind=kOutput, calls=%fused_computation.56 | convolution fusion | flops 67158016 | bytes 8495104 | tf_op jit(solution)/shard_map/dot_general | solution.py:67
  19.3 2.3 fusion.43
  22.4 19.7 %all-reduce = (f32[8]{0:T(128)S(1)}, f32[8,512]{1,0:T(8,128)S(1)}) all-reduce(f32[8]{0:T(128)S(1)} %fusion.5, f32[8,512]{1,0:T(8,128)S(1)} %fusion.30), channel_id=1, replica_groups=mesh['groups'=2,'seq'=4,'section'=2,'tp'=2] {'seq'}, use_global_device_ids=true, to_apply=%region_1.0 | all-reduce | flops 4104 | bytes 32832 | tf_op jit(solution)/shard_map/psum | solution.py:73
  42.3 1.3 copy.94
  43.6 1.3 copy.95
  44.9 10.5 %all-reduce.3.cloned.1.call-done = f32[8,2048]{1,0:T(8,128)} async-done(((f32[8,2048]{1,0:T(8,128)}), f32[8,2048]{1,0:T(8,128)}) %all-reduce.3.cloned.1.call-update) | async-done | bytes 65552 | tf_op jit(solution)/shard_map/psum | solution.py:73
  55.4 0.9 multiply_convert_fusion
  56.6 13.1 %all-gather = f32[32,2,8]{2,1,0:T(2,128)S(1)} all-gather(f32[8,2,8]{2,1,0:T(2,128)S(1)} %get-tuple-element.101), channel_id=2, replica_groups=mesh['groups'=2,'seq'=4,'section'=2,'tp'=2] {'seq'}, dimensions={0}, use_global_device_ids=true | all-gather | bytes 2560 | tf_op jit(solution)/shard_map/all_gather | solution.py:17
  70.0 13.2 %all-gather.1 = f32[32,2,8]{2,1,0:T(2,128)S(1)} all-gather(f32[8,2,8]{2,1,0:T(2,128)S(1)} %fusion.10), channel_id=3, replica_groups=mesh['groups'=2,'seq'=4,'section'=2,'tp'=2] {'seq'}, dimensions={0}, use_global_device_ids=true | all-gather | bytes 2560 | tf_op jit(solution)/shard_map/all_gather | solution.py:17
  83.6 13.8 %all-gather.2 = f32[32,2,8,128]{3,2,1,0:T(8,128)S(1)} all-gather(f32[8,2,8,128]{3,2,1,0:T(8,128)S(1)} %fusion.12), channel_id=4, replica_groups=mesh['groups'=2,'seq'=4,'section'=2,'tp'=2] {'seq'}, dimensions={0}, use_global_device_ids=true | all-gather | bytes 327680 | tf_op jit(solution)/shard_map/all_gather | solution.py:17
  98.3 5.2 %fusion.17 = f32[8,2048]{1,0:T(8,128)} fusion(bf16[2048,2048]{1,0:T(8,128)(2,1)} %param.27, bf16[1,8,16,128]{3,2,1,0:T(8,128)(2,1)S(1)} %fusion.25), kind=kOutput, calls=%fused_computation.38 | convolution fusion | flops 67108864 | bytes 8486912 | tf_op jit(solution)/shard_map/dot_general | solution.py:120
  103.6 29.5 %copy.98 = bf16[256,8,2,4096]{3,1,2,0:T(8,128)(2,1)} copy(bf16[256,8,2,4096]{3,2,1,0:T(2,128)(2,1)} %bitcast.80) | data formatting | bytes 67108864
  133.1 44.5 %copy.83 = bf16[8192,2048]{1,0:T(8,128)(2,1)} copy(bf16[8192,2048]{0,1:T(8,128)(2,1)} %bitcast.79) | data formatting | bytes 67108864 | tf_op jit(solution)/shard_map/dot_general | solution.py:130
  178.3 5.2 %all_gather.34 = bf16[8,2048]{1,0:T(8,128)(2,1)S(1)} all-gather(bf16[8,512]{1,0:T(8,128)(2,1)S(1)} %add_convert_fusion.1), channel_id=1, replica_groups=mesh['groups'=2,'seq'=4,'section'=2,'tp'=2] {'section','tp'}, dimensions={1}, use_global_device_ids=true | all-gather | bytes 40960 | tf_op jit(solution)/shard_map/all_gather | solution.py:123
  183.6 14.8 %fusion.15 = f32[8,2,4096]{2,0,1:T(8,128)} fusion(bf16[2,4096,2048]{2,1,0:T(8,128)(2,1)} %bitcast.78, bf16[8,2048]{1,0:T(8,128)(2,1)S(1)} %all_gather.34, f32[2048]{0:T(1024)S(1)} %copy-done.7), kind=kOutput, calls=%fused_computation.37 | convolution fusion | flops 268484608 | bytes 33857536 | tf_op jit(solution)/shard_map/dot_general | solution.py:130
  198.6 10.6 %psum.38 = f32[8]{0:T(128)S(1)} all-reduce(f32[8]{0:T(128)S(1)} %fusion.7), channel_id=1, replica_groups=mesh['groups'=2,'seq'=4,'section'=2,'tp'=2] {'seq'}, use_global_device_ids=true, to_apply=%region_10.11 | all-reduce | flops 8 | bytes 64 | tf_op jit(solution)/shard_map/psum | solution.py:125
  209.2 9.1 %reduce-scatter.6.cloned.1.call-done = f32[8,2,1024]{2,0,1:T(8,128)} async-done(((f32[8,2,4096]{2,0,1:T(8,128)}), f32[8,2,1024]{2,0,1:T(8,128)}) %reduce-scatter.6.cloned.1.call-update) | async-done | bytes 65552 | tf_op jit(solution)/shard_map/reduce_scatter | solution.py:133
  219.6 57.6 %psum.39 = f32[8,544]{1,0:T(8,128)S(1)} all-reduce(f32[8,544]{1,0:T(8,128)S(1)} %fusion.47), channel_id=1, replica_groups=mesh['groups'=2,'seq'=4,'section'=2,'tp'=2] {'seq','section','tp'}, use_global_device_ids=true, to_apply=%region_13.14 | all-reduce | flops 4352 | bytes 34816 | tf_op jit(solution)/shard_map/psum | solution.py:140
  277.6 1.1 multiply_reduce_fusion
  279.6 13.3 %all_gather.35 = bf16[8,4096]{1,0:T(8,128)(2,1)S(1)} all-gather(bf16[8,1024]{1,0:T(8,128)(2,1)S(1)} %multiply_convert_fusion.1), channel_id=1, replica_groups=mesh['groups'=2,'seq'=4,'section'=2,'tp'=2] {'seq'}, dimensions={1}, use_global_device_ids=true | all-gather | bytes 81920 | tf_op jit(solution)/shard_map/all_gather | solution.py:158
  292.9 8.7 %fusion.48 = f32[8,2048]{1,0:T(8,128)} fusion(bf16[8,4096]{1,0:T(8,128)(2,1)S(1)} %all_gather.35, bf16[4096,2048]{1,0:T(8,128)(2,1)} %param.37), kind=kOutput, calls=%fused_computation.82 | convolution fusion | flops 134217728 | bytes 16908288 | tf_op jit(solution)/shard_map/dot_general | solution.py:157
  302.2 16.3 %reduce-scatter.8.cloned.1.call-done = f32[8,512]{1,0:T(8,128)} async-done(((f32[8,2048]{1,0:T(8,128)}), f32[8,512]{1,0:T(8,128)}) %reduce-scatter.8.cloned.1.call-update) | async-done | bytes 16400 | tf_op jit(solution)/shard_map/reduce_scatter | solution.py:162
  318.5 1.3 add_convert_fusion
  (91 shorter events, 7.6 us)
Async XLA Ops:
  7.2 212.1 %copy-start = (bf16[1024,544]{0,1:T(8,128)(2,1)S(1)}, bf16[1024,544]{0,1:T(8,128)(2,1)}, u32[]{:S(2)}) copy-start(bf16[1024,544]{0,1:T(8,128)(2,1)} %param.32) | copy-start | bytes 3342340
  7.2 48.2 %all-reduce.3.cloned.1.call-start = ((), (), s32[]{:S(2)}) async-start(), calls=%async_computation.3 | async-start | bytes 131072 | tf_op jit(solution)/shard_map/psum | solution.py:73
  13.8 7.8 %copy-start.1 = (bf16[2048,2,256]{2,1,0:T(2,128)(2,1)S(1)}, bf16[2048,2,256]{2,1,0:T(2,128)(2,1)}, u32[]{:S(2)}) copy-start(bf16[2048,2,256]{2,1,0:T(2,128)(2,1)} %param.26) | copy-start | bytes 6291460
  13.8 8.3 %copy-start.5 = (f32[2048]{0:T(1024)S(1)}, f32[2048]{0:T(1024)}, u32[]{:S(2)}) copy-start(f32[2048]{0:T(1024)} %param.24) | copy-start | bytes 24580
  13.8 28.4 %copy-start.13 = (s32[8]{0:T(128)S(1)}, s32[8]{0:T(128)}, u32[]{:S(2)}) copy-start(s32[8]{0:T(128)} %param.22) | copy-start | bytes 100
  19.2 158.4 %reduce-scatter.4.cloned.1.call-start = ((), (), s32[]{:S(2)}) async-start(), calls=%async_computation.4 | async-start | bytes 81920 | tf_op jit(solution)/shard_map/reduce_scatter | solution.py:121
  103.6 114.8 %reduce-scatter.6.cloned.1.call-start = ((), (), s32[]{:S(2)}) async-start(), calls=%async_computation.5 | async-start | bytes 327680 | tf_op jit(solution)/shard_map/reduce_scatter | solution.py:133
  133.1 44.5 %copy-start.8 = (bf16[8,512]{1,0:T(8,128)(2,1)S(1)}, bf16[8,512]{1,0:T(8,128)(2,1)}, u32[]{:S(2)}) copy-start(bf16[8,512]{1,0:T(8,128)(2,1)} %param.21) | copy-start | bytes 24580
  133.1 50.4 %copy-start.7 = (f32[2048]{0:T(1024)S(1)}, f32[2048]{0:T(1024)}, u32[]{:S(2)}) copy-start(f32[2048]{0:T(1024)} %param.28) | copy-start | bytes 24580
  183.5 15.1 %copy-start.6 = (f32[16,1024]{1,0:T(8,128)S(1)}, f32[16,1024]{1,0:T(8,128)}, u32[]{:S(2)}) copy-start(f32[16,1024]{1,0:T(8,128)} %param.35) | copy-start | bytes 196612
  183.5 35.7 %copy-start.4 = (bf16[8,3,1024]{2,0,1:T(8,128)(2,1)S(1)}, bf16[8,3,1024]{2,0,1:T(8,128)(2,1)}, u32[]{:S(2)}) copy-start(bf16[8,3,1024]{2,0,1:T(8,128)(2,1)} %param.39) | copy-start | bytes 147460
  183.5 35.7 %copy-start.9 = (f32[4,1024]{1,0:T(4,128)S(1)}, f32[4,1024]{1,0:T(4,128)}, u32[]{:S(2)}) copy-start(f32[4,1024]{1,0:T(4,128)} %param.30) | copy-start | bytes 49156
  183.5 35.7 %copy-start.12 = (f32[1024]{0:T(1024)S(1)}, f32[1024]{0:T(1024)}, u32[]{:S(2)}) copy-start(f32[1024]{0:T(1024)} %param.31) | copy-start | bytes 12292
  183.5 93.8 %copy-start.2 = (bf16[512,1024]{1,0:T(8,128)(2,1)S(1)}, bf16[512,1024]{1,0:T(8,128)(2,1)}, u32[]{:S(2)}) copy-start(bf16[512,1024]{1,0:T(8,128)(2,1)} %param.33) | copy-start | bytes 3145732
  183.5 93.8 %copy-start.10 = (f32[1024]{0:T(1024)S(1)}, f32[1024]{0:T(1024)}, u32[]{:S(2)}) copy-start(f32[1024]{0:T(1024)} %param.34) | copy-start | bytes 12292
  183.6 94.1 %copy-start.3 = (f32[8,16,1024]{2,1,0:T(8,128)S(1)}, f32[8,16,1024]{2,1,0:T(8,128)}, u32[]{:S(2)}) copy-start(f32[8,16,1024]{2,1,0:T(8,128)} %param.38) | copy-start | bytes 1572868
  183.6 95.2 %copy-start.11 = (f32[1024]{0:T(1024)S(1)}, f32[1024]{0:T(1024)}, u32[]{:S(2)}) copy-start(f32[1024]{0:T(1024)} %param.36) | copy-start | bytes 12292
  198.4 120.1 %reduce-scatter.8.cloned.1.call-start = ((), (), s32[]{:S(2)}) async-start(), calls=%async_computation.6 | async-start | bytes 81920 | tf_op jit(solution)/shard_map/reduce_scatter | solution.py:162
Sparse Core Ops, SparseCore 0:
  19.3 36.0 all-reduce.2
  103.7 19.3 reduce-scatter.3
  198.5 19.7 reduce-scatter.5
  301.7 16.7 reduce-scatter.7
where the time goes:
time: 328 us; the launch traced here: 326 us
  blocking collectives  153 us (47%)
  local copies, waits for them, and re-layouts  79.6 us (24%)
  waiting for transfers between devices  36 us (11%)
  matrix products  35.9 us (11%)
  between operations  14 us (4%)
  other arithmetic  7.51 us (2%)
    psum x1, blocking collectives, on_device(): lax.psum(jnp.dot(conv_act, w_xproj, preferred_element_type=jnp.float32),...  57.6 us
    dot_general x1, local copies, waits for them, and re-layouts, on_device(): jnp.dot(scaled_mid, w_inproj.reshape(in_rows, 2 * local_inner), preferred...  44.5 us
    all_gather x3, blocking collectives, joined(): pieces = jax.tree.map(lambda part: lax.all_gather(part, axis), value)  40.1 us
    unnamed x32, local copies, waits for them, and re-layouts  32.7 us
    psum x1, blocking collectives, on_device(): lax.psum((square_part, query_part, keyval_part), 'seq')  19.7 us
    reduce_scatter x1, waiting for transfers between devices, on_device(): lax.psum_scatter(mamba_part, ('section', 'tp'), scatter_dimension=1, tile...  16.3 us
    dot_general x1, matrix products, on_device(): jnp.dot(scaled_mid, w_inproj.reshape(in_rows, 2 * local_inner), preferred...  14.8 us
    all_gather x1, blocking collectives, on_device(): lax.all_gather(gated_out, 'seq', axis=1, tiled=True)  13.3 us
  transfers between devices with their start and end apart: 4, of which 3 were waited for; matrix products, arithmetic and copies ran while one was open for 25% of the time, Pallas kernels for 0%

commit v1 on v0

--- a/solution.py
+++ b/solution.py
@@ -137,9 +137,9 @@
     window = jnp.concatenate([conv_window, conv_input[:, None, :]], axis=1)
     conv_out = conv_bias + jnp.sum(conv_weight[None] * window.astype(jnp.float32), axis=1)
     conv_act = jax.nn.silu(conv_out).astype(jnp.bfloat16)
-    xproj_out = lax.psum(
-        jnp.dot(conv_act, w_xproj, preferred_element_type=jnp.float32), ("seq", "section", "tp")
-    )
+    own = jnp.dot(conv_act, w_xproj, preferred_element_type=jnp.float32)
+    terms = lax.all_gather(own, ("seq", "section", "tp"), axis=0, tiled=False)
+    xproj_out = terms.sum(axis=0)
     rate_low = xproj_out[:, :DTR].astype(jnp.bfloat16)
     input_proj = xproj_out[:, DTR : DTR + DS]
     output_proj = xproj_out[:, DTR + DS :]

time: 328 us -> 290 us (0.88)
  blocking collectives: 153 us -> 115 us
    psum x1 -> x0, blocking collectives: 57.6 us -> none  [on_device(): lax.psum(jnp.dot(conv_act, w_xproj, preferred_element_type=jnp.float32),...]
    all_gather x0 -> x1, blocking collectives: none -> 19.4 us  [on_device(): terms = lax.all_gather(own, ('seq', 'section', 'tp'), axis=0, tiled=False)]
  transfers between devices with their start and end apart: 4 -> 4, of which waited for: 3 -> 3; matrix products, arithmetic and copies ran while one was open for 25% -> 28% of each run, Pallas kernels for 0% -> 0%
where the time goes in v1:
time: 290 us; the launch traced here: 288 us
  blocking collectives  115 us (40%)
  local copies, waits for them, and re-layouts  79.6 us (27%)
  waiting for transfers between devices  36.1 us (12%)
  matrix products  35.9 us (12%)
  between operations  14 us (5%)
  other arithmetic  7.54 us (3%)
    dot_general x1, local copies, waits for them, and re-layouts, on_device(): jnp.dot(scaled_mid, w_inproj.reshape(in_rows, 2 * local_inner), preferred...  44.5 us
    all_gather x3, blocking collectives, joined(): pieces = jax.tree.map(lambda part: lax.all_gather(part, axis), value)  40.1 us
    unnamed x32, local copies, waits for them, and re-layouts  32.7 us
    psum x1, blocking collectives, on_device(): lax.psum((square_part, query_part, keyval_part), 'seq')  19.7 us
    all_gather x1, blocking collectives, on_device(): terms = lax.all_gather(own, ('seq', 'section', 'tp'), axis=0, tiled=False)  19.4 us
    reduce_scatter x1, waiting for transfers between devices, on_device(): lax.psum_scatter(mamba_part, ('section', 'tp'), scatter_dimension=1, tile...  16.4 us
    dot_general x1, matrix products, on_device(): jnp.dot(scaled_mid, w_inproj.reshape(in_rows, 2 * local_inner), preferred...  14.8 us
    all_gather x1, blocking collectives, on_device(): lax.all_gather(gated_out, 'seq', axis=1, tiled=True)  13.3 us
  transfers between devices with their start and end apart: 4, of which 3 were waited for; matrix products, arithmetic and copies ran while one was open for 28% of the time, Pallas kernels for 0%

profile of v1, /device:TPU:0, one launch (start us, length us, event | category | flops | bytes accessed | tf_op | source)
XLA Modules:
  0.0 288.3 jit_solution(14254712098349582015)
XLA Ops:
  7.2 6.5 %all_gather.33 = bf16[8,2048]{1,0:T(8,128)(2,1)S(1)} all-gather(bf16[8,512]{1,0:T(8,128)(2,1)} %param.21), channel_id=1, replica_groups=mesh['groups'=2,'seq'=4,'section'=2,'tp'=2] {'section','tp'}, dimensions={1}, use_global_device_ids=true | all-gather | bytes 40960 | tf_op jit(solution)/shard_map/all_gather | solution.py:63
  13.8 5.4 %fusion.32 = f32[8,2048]{1,0:T(8,128)} fusion(bf16[2048,2048]{1,0:T(8,128)(2,1)} %param.25, bf16[8,2048]{1,0:T(8,128)(2,1)S(1)} %all_gather.33, f32[2048]{0:T(1024)} %param.24), kind=kOutput, calls=%fused_computation.57 | convolution fusion | flops 67158016 | bytes 8495104 | tf_op jit(solution)/shard_map/dot_general | solution.py:67
  19.3 2.3 fusion.43
  22.4 19.7 %all-reduce = (f32[8]{0:T(128)S(1)}, f32[8,512]{1,0:T(8,128)S(1)}) all-reduce(f32[8]{0:T(128)S(1)} %fusion.5, f32[8,512]{1,0:T(8,128)S(1)} %fusion.30), channel_id=1, replica_groups=mesh['groups'=2,'seq'=4,'section'=2,'tp'=2] {'seq'}, use_global_device_ids=true, to_apply=%region_1.0 | all-reduce | flops 4104 | bytes 32832 | tf_op jit(solution)/shard_map/psum | solution.py:73
  42.3 1.3 copy.94
  43.6 1.3 copy.95
  44.9 10.5 %all-reduce.3.cloned.1.call-done = f32[8,2048]{1,0:T(8,128)} async-done(((f32[8,2048]{1,0:T(8,128)}), f32[8,2048]{1,0:T(8,128)}) %all-reduce.3.cloned.1.call-update) | async-done | bytes 65552 | tf_op jit(solution)/shard_map/psum | solution.py:73
  55.4 0.9 multiply_convert_fusion
  56.6 13.1 %all-gather = f32[32,2,8]{2,1,0:T(2,128)S(1)} all-gather(f32[8,2,8]{2,1,0:T(2,128)S(1)} %get-tuple-element.101), channel_id=2, replica_groups=mesh['groups'=2,'seq'=4,'section'=2,'tp'=2] {'seq'}, dimensions={0}, use_global_device_ids=true | all-gather | bytes 2560 | tf_op jit(solution)/shard_map/all_gather | solution.py:17
  70.0 13.2 %all-gather.1 = f32[32,2,8]{2,1,0:T(2,128)S(1)} all-gather(f32[8,2,8]{2,1,0:T(2,128)S(1)} %fusion.10), channel_id=3, replica_groups=mesh['groups'=2,'seq'=4,'section'=2,'tp'=2] {'seq'}, dimensions={0}, use_global_device_ids=true | all-gather | bytes 2560 | tf_op jit(solution)/shard_map/all_gather | solution.py:17
  83.6 13.8 %all-gather.2 = f32[32,2,8,128]{3,2,1,0:T(8,128)S(1)} all-gather(f32[8,2,8,128]{3,2,1,0:T(8,128)S(1)} %fusion.12), channel_id=4, replica_groups=mesh['groups'=2,'seq'=4,'section'=2,'tp'=2] {'seq'}, dimensions={0}, use_global_device_ids=true | all-gather | bytes 327680 | tf_op jit(solution)/shard_map/all_gather | solution.py:17
  98.3 5.2 %fusion.17 = f32[8,2048]{1,0:T(8,128)} fusion(bf16[2048,2048]{1,0:T(8,128)(2,1)} %param.27, bf16[1,8,16,128]{3,2,1,0:T(8,128)(2,1)S(1)} %fusion.25), kind=kOutput, calls=%fused_computation.39 | convolution fusion | flops 67108864 | bytes 8486912 | tf_op jit(solution)/shard_map/dot_general | solution.py:120
  103.6 29.5 %copy.98 = bf16[256,8,2,4096]{3,1,2,0:T(8,128)(2,1)} copy(bf16[256,8,2,4096]{3,2,1,0:T(2,128)(2,1)} %bitcast.82) | data formatting | bytes 67108864
  133.1 44.5 %copy.83 = bf16[8192,2048]{1,0:T(8,128)(2,1)} copy(bf16[8192,2048]{0,1:T(8,128)(2,1)} %bitcast.81) | data formatting | bytes 67108864 | tf_op jit(solution)/shard_map/dot_general | solution.py:130
  178.3 5.2 %all_gather.40 = bf16[8,2048]{1,0:T(8,128)(2,1)S(1)} all-gather(bf16[8,512]{1,0:T(8,128)(2,1)S(1)} %add_convert_fusion.1), channel_id=1, replica_groups=mesh['groups'=2,'seq'=4,'section'=2,'tp'=2] {'section','tp'}, dimensions={1}, use_global_device_ids=true | all-gather | bytes 40960 | tf_op jit(solution)/shard_map/all_gather | solution.py:123
  183.6 14.8 %fusion.15 = f32[8,2,4096]{2,0,1:T(8,128)} fusion(bf16[2,4096,2048]{2,1,0:T(8,128)(2,1)} %bitcast.80, bf16[8,2048]{1,0:T(8,128)(2,1)S(1)} %all_gather.40, f32[2048]{0:T(1024)S(1)} %copy-done.7), kind=kOutput, calls=%fused_computation.38 | convolution fusion | flops 268484608 | bytes 33857536 | tf_op jit(solution)/shard_map/dot_general | solution.py:130
  198.6 10.6 %psum.31 = f32[8]{0:T(128)S(1)} all-reduce(f32[8]{0:T(128)S(1)} %fusion.7), channel_id=1, replica_groups=mesh['groups'=2,'seq'=4,'section'=2,'tp'=2] {'seq'}, use_global_device_ids=true, to_apply=%region_10.11 | all-reduce | flops 8 | bytes 64 | tf_op jit(solution)/shard_map/psum | solution.py:125
  209.2 9.1 %reduce-scatter.6.cloned.1.call-done = f32[8,2,1024]{2,0,1:T(8,128)} async-done(((f32[8,2,4096]{2,0,1:T(8,128)}), f32[8,2,1024]{2,0,1:T(8,128)}) %reduce-scatter.6.cloned.1.call-update) | async-done | bytes 65552 | tf_op jit(solution)/shard_map/reduce_scatter | solution.py:133
  219.6 19.4 %all-gather.3 = f32[128,544]{1,0:T(8,128)S(1)} all-gather(f32[8,544]{1,0:T(8,128)S(1)} %fusion.47), channel_id=5, replica_groups=mesh['groups'=2,'seq'=4,'section'=2,'tp'=2] {'seq','section','tp'}, dimensions={0}, use_global_device_ids=true | all-gather | bytes 295936 | tf_op jit(solution)/shard_map/all_gather | solution.py:141
  239.5 1.1 multiply_reduce_fusion
  241.4 13.3 %all_gather.43 = bf16[8,4096]{1,0:T(8,128)(2,1)S(1)} all-gather(bf16[8,1024]{1,0:T(8,128)(2,1)S(1)} %multiply_convert_fusion.1), channel_id=1, replica_groups=mesh['groups'=2,'seq'=4,'section'=2,'tp'=2] {'seq'}, dimensions={1}, use_global_device_ids=true | all-gather | bytes 81920 | tf_op jit(solution)/shard_map/all_gather | solution.py:158
  254.7 8.7 %fusion.48 = f32[8,2048]{1,0:T(8,128)} fusion(bf16[8,4096]{1,0:T(8,128)(2,1)S(1)} %all_gather.43, bf16[4096,2048]{1,0:T(8,128)(2,1)} %param.37), kind=kOutput, calls=%fused_computation.83 | convolution fusion | flops 134217728 | bytes 16908288 | tf_op jit(solution)/shard_map/dot_general | solution.py:157
  264.0 16.4 %reduce-scatter.8.cloned.1.call-done = f32[8,512]{1,0:T(8,128)} async-done(((f32[8,2048]{1,0:T(8,128)}), f32[8,512]{1,0:T(8,128)}) %reduce-scatter.8.cloned.1.call-update) | async-done | bytes 16400 | tf_op jit(solution)/shard_map/reduce_scatter | solution.py:162
  280.5 1.3 add_convert_fusion
  (92 shorter events, 7.7 us)
Async XLA Ops:
  7.2 212.1 %copy-start = (bf16[1024,544]{0,1:T(8,128)(2,1)S(1)}, bf16[1024,544]{0,1:T(8,128)(2,1)}, u32[]{:S(2)}) copy-start(bf16[1024,544]{0,1:T(8,128)(2,1)} %param.32) | copy-start | bytes 3342340
  7.2 48.2 %all-reduce.3.cloned.1.call-start = ((), (), s32[]{:S(2)}) async-start(), calls=%async_computation.3 | async-start | bytes 131072 | tf_op jit(solution)/shard_map/psum | solution.py:73
  13.8 7.8 %copy-start.1 = (bf16[2048,2,256]{2,1,0:T(2,128)(2,1)S(1)}, bf16[2048,2,256]{2,1,0:T(2,128)(2,1)}, u32[]{:S(2)}) copy-start(bf16[2048,2,256]{2,1,0:T(2,128)(2,1)} %param.26) | copy-start | bytes 6291460
  13.8 8.3 %copy-start.5 = (f32[2048]{0:T(1024)S(1)}, f32[2048]{0:T(1024)}, u32[]{:S(2)}) copy-start(f32[2048]{0:T(1024)} %param.24) | copy-start | bytes 24580
  13.8 28.4 %copy-start.13 = (s32[8]{0:T(128)S(1)}, s32[8]{0:T(128)}, u32[]{:S(2)}) copy-start(s32[8]{0:T(128)} %param.22) | copy-start | bytes 100
  19.2 158.4 %reduce-scatter.4.cloned.1.call-start = ((), (), s32[]{:S(2)}) async-start(), calls=%async_computation.4 | async-start | bytes 81920 | tf_op jit(solution)/shard_map/reduce_scatter | solution.py:121
  103.6 114.8 %reduce-scatter.6.cloned.1.call-start = ((), (), s32[]{:S(2)}) async-start(), calls=%async_computation.5 | async-start | bytes 327680 | tf_op jit(solution)/shard_map/reduce_scatter | solution.py:133
  133.1 44.5 %copy-start.8 = (bf16[8,512]{1,0:T(8,128)(2,1)S(1)}, bf16[8,512]{1,0:T(8,128)(2,1)}, u32[]{:S(2)}) copy-start(bf16[8,512]{1,0:T(8,128)(2,1)} %param.21) | copy-start | bytes 24580
  133.1 50.4 %copy-start.7 = (f32[2048]{0:T(1024)S(1)}, f32[2048]{0:T(1024)}, u32[]{:S(2)}) copy-start(f32[2048]{0:T(1024)} %param.28) | copy-start | bytes 24580
  183.5 15.1 %copy-start.6 = (f32[16,1024]{1,0:T(8,128)S(1)}, f32[16,1024]{1,0:T(8,128)}, u32[]{:S(2)}) copy-start(f32[16,1024]{1,0:T(8,128)} %param.35) | copy-start | bytes 196612
  183.5 35.7 %copy-start.4 = (bf16[8,3,1024]{2,0,1:T(8,128)(2,1)S(1)}, bf16[8,3,1024]{2,0,1:T(8,128)(2,1)}, u32[]{:S(2)}) copy-start(bf16[8,3,1024]{2,0,1:T(8,128)(2,1)} %param.39) | copy-start | bytes 147460
  183.5 35.7 %copy-start.9 = (f32[4,1024]{1,0:T(4,128)S(1)}, f32[4,1024]{1,0:T(4,128)}, u32[]{:S(2)}) copy-start(f32[4,1024]{1,0:T(4,128)} %param.30) | copy-start | bytes 49156
  183.5 35.7 %copy-start.12 = (f32[1024]{0:T(1024)S(1)}, f32[1024]{0:T(1024)}, u32[]{:S(2)}) copy-start(f32[1024]{0:T(1024)} %param.31) | copy-start | bytes 12292
  183.5 55.7 %copy-start.2 = (bf16[512,1024]{1,0:T(8,128)(2,1)S(1)}, bf16[512,1024]{1,0:T(8,128)(2,1)}, u32[]{:S(2)}) copy-start(bf16[512,1024]{1,0:T(8,128)(2,1)} %param.33) | copy-start | bytes 3145732
  183.5 55.6 %copy-start.10 = (f32[1024]{0:T(1024)S(1)}, f32[1024]{0:T(1024)}, u32[]{:S(2)}) copy-start(f32[1024]{0:T(1024)} %param.34) | copy-start | bytes 12292
  183.6 55.9 %copy-start.3 = (f32[8,16,1024]{2,1,0:T(8,128)S(1)}, f32[8,16,1024]{2,1,0:T(8,128)}, u32[]{:S(2)}) copy-start(f32[8,16,1024]{2,1,0:T(8,128)} %param.38) | copy-start | bytes 1572868
  183.6 57.0 %copy-start.11 = (f32[1024]{0:T(1024)S(1)}, f32[1024]{0:T(1024)}, u32[]{:S(2)}) copy-start(f32[1024]{0:T(1024)} %param.36) | copy-start | bytes 12292
  198.4 82.1 %reduce-scatter.8.cloned.1.call-start = ((), (), s32[]{:S(2)}) async-start(), calls=%async_computation.6 | async-start | bytes 81920 | tf_op jit(solution)/shard_map/reduce_scatter | solution.py:162
Sparse Core Ops, SparseCore 0:
  19.3 36.0 all-reduce.2
  103.7 19.3 reduce-scatter.3
  198.5 19.7 reduce-scatter.5
  263.5 16.8 reduce-scatter.7
